TPU v7x, 256 devices: a whole 4x4x8 slice. The times are simulated.
256 devices in a mesh: grp: 16 (over x, z_lo, core), row: 4 (over z_hi), col: 4 (over y).
Axes of the slice: x: 4, y: 4, z: 8 (z_hi: 4, z_lo: 2; z = z_hi * 2 + z_lo), core: 2. Of those that a mesh axis runs over, the one named last changes fastest.
Arguments:
- volume: float32 [32, 32, 32, 512], P(None, 'grp', 'row', 'col'), may hold values from -6 to 6
- forcing: float32 [32, 32, 32, 512], P(None, 'grp', 'row', 'col'), may hold values from -6 to 6
- medium: float32 [2, 32, 32, 512], P(None, 'grp', 'row', 'col'), may hold values from 0.5 to 3
- points: float32 [3, 32768], P(None, ('grp', 'row', 'col')), may hold values from 0 to 4
- weights: float32 [32768], P(('grp', 'row', 'col')), may hold values from 0.05 to 0.5
- cell_map: int32 [32768], P(('grp', 'row', 'col')), may hold values from 0 to 2047
- near_list: int32 [256, 256], replicated, may hold values from 0 to 1, as said below
Outputs:
- new_volume: float32 [32, 32, 32, 512], P(None, 'grp', 'row', 'col')
- potential: float32 [32, 32768], P(None, ('grp', 'row', 'col'))
Inputs may be any that keep to these rules, and one draw needn't show every extreme that they name: cell_map[p] numbers a cell of tile p // 128 in row-major order of the tile's 2 x 8 x 128 cells. near_list[i, j] = 1 lists cluster j as near to cluster i; every cluster lists itself, and how many clusters a cluster lists differs from cluster to cluster.
All inputs are finite; a program needn't handle non-finite values.
Results may differ from a plain program's by a relative error of at most 0.0041.
Values may be sent and summed in bfloat16 or wider, within the bound.
No kernel may reach another device: no remote copies, remote signals or barrier semaphores. Data moves between devices by JAX's collectives and lax.ppermute only.
A program may use at most 64 MiB of HBM per device.

v0:
```python
import jax
import jax.numpy as jnp
from jax import lax
from jax.sharding import PartitionSpec as P

RHS = 16
CX = 2
CY = 8
CZ = 128
CH = 32
FOUR_PI = 4.0 * 3.141592653589793
WAVENUMBER = 10.0
SOFTENING = 0.01
RELAX_RATE = 0.8
COUPLING = 0.5
CONTRACT = (((1,), (1,)), ((), ()))


def padded_2(x, sides, width):
    for axis, dim in sides:
        size, length = (lax.axis_size(axis), x.shape[dim])
        up = [(i, (i + 1) % size) for i in range(size - 1)]
        down = [(j, i) for i, j in up]
        last = lax.slice_in_dim(x, length - width, length, axis=dim)
        first = lax.slice_in_dim(x, 0, width, axis=dim)
        before = lax.ppermute(last, axis, up)
        after = lax.ppermute(first, axis, down)
        x = jnp.concatenate([before, x, after], axis=dim)
    return x


def helmholtz(volume, medium):
    padded = padded_2(volume, (("grp", 1), ("row", 2), ("col", 3)), 1)
    beside = padded[:, 2:, 1:-1, 1:-1] + padded[:, :-2, 1:-1, 1:-1]
    beside = beside + padded[:, 1:-1, 2:, 1:-1] + padded[:, 1:-1, :-2, 1:-1]
    beside = beside + padded[:, 1:-1, 1:-1, 2:] + padded[:, 1:-1, 1:-1, :-2]
    laplace = 6.0 * volume - beside
    real_in = volume[:RHS]
    imag_in = volume[RHS:]
    real_out = laplace[:RHS] - medium[0] * real_in + medium[1] * imag_in
    imag_out = laplace[RHS:] - medium[0] * imag_in - medium[1] * real_in
    return jnp.concatenate([real_out, imag_out], 0)


def kernel_tiles(targets, sources, listed):
    delta_x = targets[0][:, None] - sources[0][None, :]
    delta_y = targets[1][:, None] - sources[1][None, :]
    delta_z = targets[2][:, None] - sources[2][None, :]
    distance = jnp.sqrt(delta_x * delta_x + delta_y * delta_y + delta_z * delta_z + SOFTENING)
    factor = listed / (FOUR_PI * distance)
    tile_real = (jnp.cos(WAVENUMBER * distance) * factor).astype(jnp.bfloat16)
    tile_imag = (jnp.sin(WAVENUMBER * distance) * factor).astype(jnp.bfloat16)
    return (tile_real, tile_imag)


def complex_product(real_sum, imag_sum):
    return jnp.concatenate([real_sum[:RHS] - imag_sum[RHS:], real_sum[RHS:] + imag_sum[:RHS]], 0)


def block_clusters(clusters, cluster_size, limit):
    chosen = 1
    for trial in range(1, clusters + 1):
        if clusters % trial == 0 and trial * cluster_size <= limit:
            chosen = trial
    return chosen


def on_device(volume, forcing, medium, points, weights, cell_map, near_list):
    residual = forcing - helmholtz(volume, medium)
    relaxed = volume + RELAX_RATE * residual / (6.0 - medium[0])[None]
    flat = relaxed.reshape(CH, CX * CY * CZ)
    traces = (jnp.take(flat, cell_map, axis=1) * weights[None, :]).astype(jnp.bfloat16)
    group_count = lax.axis_size("grp") * lax.axis_size("row")
    column_count = lax.axis_size("col")
    group_index = lax.axis_index("grp") * lax.axis_size("row") + lax.axis_index("row")
    column_index = lax.axis_index("col")
    near_blocks = near_list.reshape(group_count, column_count, group_count, column_count)
    cluster = points.shape[1]
    own_cols = lax.dynamic_index_in_dim(near_blocks, column_index, 1, keepdims=False)
    own_cols = lax.dynamic_index_in_dim(own_cols, group_index, 1, keepdims=False)
    targets = lax.all_gather(points, ("grp", "row"), axis=1, tiled=True)
    sources = lax.all_gather(points, "col", axis=1, tiled=True)
    source_traces = lax.all_gather(traces, "col", axis=1, tiled=True)
    target_count = targets.shape[1]
    source_count = sources.shape[1]
    step_clusters = block_clusters(group_count, cluster, 1024)
    block_points = step_clusters * cluster

    def one_block(turn, partial_value):
        begin = turn * block_points
        block_targets = lax.dynamic_slice_in_dim(targets, begin, block_points, 1)
        flags = lax.dynamic_slice_in_dim(own_cols, turn * step_clusters, step_clusters, 0)
        listed = jnp.broadcast_to(
            flags[:, None, :, None].astype(jnp.float32),
            (step_clusters, cluster, column_count, cluster),
        )
        listed = listed.reshape(block_points, source_count)
        tile_real, tile_imag = kernel_tiles(block_targets, sources, listed)
        real_part = lax.dot_general(
            source_traces, tile_real, CONTRACT, preferred_element_type=jnp.float32
        )
        imag_part = lax.dot_general(
            source_traces, tile_imag, CONTRACT, preferred_element_type=jnp.float32
        )
        return lax.dynamic_update_slice_in_dim(
            partial_value, complex_product(real_part, imag_part), begin, 1
        )

    partial_value = lax.fori_loop(
        0, group_count // step_clusters, one_block, jnp.zeros((CH, target_count), jnp.float32)
    )
    potential = lax.psum_scatter(partial_value, ("grp", "row"), scatter_dimension=1, tiled=True)
    spread = jnp.zeros((CH, CX * CY * CZ), jnp.float32).at[:, cell_map].add(potential)
    new_volume = relaxed + COUPLING * spread.reshape(relaxed.shape)
    return (new_volume, potential)


def solution(mesh):
    return jax.shard_map(
        on_device,
        mesh=mesh,
        in_specs=(
            P(None, "grp", "row", "col"),
            P(None, "grp", "row", "col"),
            P(None, "grp", "row", "col"),
            P(None, ("grp", "row", "col")),
            P(("grp", "row", "col")),
            P(("grp", "row", "col")),
            P(),
        ),
        out_specs=(P(None, "grp", "row", "col"), P(None, ("grp", "row", "col"))),
        check_vma=False,
    )
```

profile of v0, /device:TPU:24, one launch (start us, length us, event | category | flops | bytes accessed | tf_op | source)
XLA Modules:
  0.0 649.2 jit_solution(6016588470859238868)
XLA Ops:
  8.2 1.7 collective-permute-start.1
  14.5 10.9 %reshape.33 = s32[64,4,64,4]{3,2,1,0:T(8,128)} reshape(s32[256,256]{1,0:T(8,128)} %param.15) | data formatting | bytes 524288 | tf_op jit(solution)/shard_map/reshape | solution.py:77
  25.4 1.6 constant_dynamic-slice_fusion.1
  29.3 5.8 collective-permute-start.3
  37.9 3.2 collective-permute-start.4
  42.4 140.7 %all_gather.9 = f32[3,8192]{1,0:T(4,128)} all-gather(f32[3,128]{1,0:T(4,128)S(1)} %copy-done.7), channel_id=1, replica_groups=mesh['grp'=16,'row'=4,'col'=4] {'grp','row'}, dimensions={1}, use_global_device_ids=true | all-gather | bytes 99840 | tf_op jit(solution)/shard_map/all_gather | solution.py:81
  185.3 10.3 %all_gather.10 = f32[3,512]{1,0:T(4,128)S(1)} all-gather(f32[3,128]{1,0:T(4,128)} %param.12), channel_id=1, replica_groups=mesh['grp'=16,'row'=4,'col'=4] {'col'}, dimensions={1}, use_global_device_ids=true | all-gather | bytes 7680 | tf_op jit(solution)/shard_map/all_gather | solution.py:82
  195.7 2.3 copy.89
  198.0 2.3 copy.90
  200.2 2.9 fusion.7
  206.7 12.0 %all_gather.11 = bf16[32,512]{0,1:T(8,128)(2,1)S(1)} all-gather(bf16[32,128]{0,1:T(8,128)(2,1)S(1)} %fusion.16), channel_id=1, replica_groups=mesh['grp'=16,'row'=4,'col'=4] {'col'}, dimensions={1}, use_global_device_ids=true | all-gather | bytes 40960 | tf_op jit(solution)/shard_map/all_gather | solution.py:83
  218.8 158.8 %while.13 = (s32[]{:T(128)}, f32[32,8192]{1,0:T(8,128)S(1)}, f32[3,8192]{1,0:T(4,128)}, f32[3,512]{1,0:T(4,128)S(1)}, s32[64,4]{0,1:T(4,128)S(1)}, /*index=5*/bf...) while((s32[]{:T(128)}, f32[32,8192]{1,0:T(8,128)S(1)}, ...), condition=%wide.region_1.2_spmd, body=%wide.region_0.1_spmd.sunk | while | flops 85524528 | bytes 11561869 | solution.py:109
  220.5 1.4 bitcast_divide_fusion.2
  221.8 8.4 %convolution_bitcast_fusion.5 = f32[32,1024]{1,0:T(8,128)S(1)} fusion(bf16[32,512]{1,0:T(8,128)(2,1)S(1)} %get-tuple-element.270, f32[1024,512]{1,0:T(8,128)S(1)} %bitcast_divide_fusion.2, f32[512]{0:T(512)S(1)} %bitcast.68, f32[1024]{0:T(1024)S(1)} %bitcast.62, f32[512]{0:T(512)S(1)} %bitcast.71, f32[1024]{0:T(1024)S(1)} %bitcast.59, ...), kind=kOutput, calls=%fused_computation.7.clone.1 | convolution fusion | flops 39845888 | bytes 2279424 | tf_op jit(solution)/shard_map/while/body/eval_jaxpr/dot_general | solution.py:99
  230.2 8.5 %convolution_bitcast_fusion.4 = f32[32,1024]{1,0:T(8,128)S(1)} fusion(bf16[32,512]{1,0:T(8,128)(2,1)S(1)} %get-tuple-element.270, f32[1024,512]{1,0:T(8,128)S(1)} %bitcast_divide_fusion.2, f32[512]{0:T(512)S(1)} %bitcast.69, f32[1024]{0:T(1024)S(1)} %bitcast.63, f32[512]{0:T(512)S(1)} %bitcast.72, f32[1024]{0:T(1024)S(1)} %bitcast.60, ...), kind=kOutput, calls=%fused_computation.6.clone.1 | convolution fusion | flops 39845888 | bytes 2279424 | tf_op jit(solution)/shard_map/while/body/eval_jaxpr/dot_general | solution.py:102
  240.3 1.4 bitcast_divide_fusion.2
  241.7 8.4 %convolution_bitcast_fusion.5 = f32[32,1024]{1,0:T(8,128)S(1)} fusion(bf16[32,512]{1,0:T(8,128)(2,1)S(1)} %get-tuple-element.270, f32[1024,512]{1,0:T(8,128)S(1)} %bitcast_divide_fusion.2, f32[512]{0:T(512)S(1)} %bitcast.68, f32[1024]{0:T(1024)S(1)} %bitcast.62, f32[512]{0:T(512)S(1)} %bitcast.71, f32[1024]{0:T(1024)S(1)} %bitcast.59, ...), kind=kOutput, calls=%fused_computation.7.clone.1 | convolution fusion | flops 39845888 | bytes 2279424 | tf_op jit(solution)/shard_map/while/body/eval_jaxpr/dot_general | solution.py:99
  250.1 8.5 %convolution_bitcast_fusion.4 = f32[32,1024]{1,0:T(8,128)S(1)} fusion(bf16[32,512]{1,0:T(8,128)(2,1)S(1)} %get-tuple-element.270, f32[1024,512]{1,0:T(8,128)S(1)} %bitcast_divide_fusion.2, f32[512]{0:T(512)S(1)} %bitcast.69, f32[1024]{0:T(1024)S(1)} %bitcast.63, f32[512]{0:T(512)S(1)} %bitcast.72, f32[1024]{0:T(1024)S(1)} %bitcast.60, ...), kind=kOutput, calls=%fused_computation.6.clone.1 | convolution fusion | flops 39845888 | bytes 2279424 | tf_op jit(solution)/shard_map/while/body/eval_jaxpr/dot_general | solution.py:102
  261.5 8.4 %convolution_bitcast_fusion.5 = f32[32,1024]{1,0:T(8,128)S(1)} fusion(bf16[32,512]{1,0:T(8,128)(2,1)S(1)} %get-tuple-element.270, f32[1024,512]{1,0:T(8,128)S(1)} %bitcast_divide_fusion.2, f32[512]{0:T(512)S(1)} %bitcast.68, f32[1024]{0:T(1024)S(1)} %bitcast.62, f32[512]{0:T(512)S(1)} %bitcast.71, f32[1024]{0:T(1024)S(1)} %bitcast.59, ...), kind=kOutput, calls=%fused_computation.7.clone.1 | convolution fusion | flops 39845888 | bytes 2279424 | tf_op jit(solution)/shard_map/while/body/eval_jaxpr/dot_general | solution.py:99
  269.9 8.5 %convolution_bitcast_fusion.4 = f32[32,1024]{1,0:T(8,128)S(1)} fusion(bf16[32,512]{1,0:T(8,128)(2,1)S(1)} %get-tuple-element.270, f32[1024,512]{1,0:T(8,128)S(1)} %bitcast_divide_fusion.2, f32[512]{0:T(512)S(1)} %bitcast.69, f32[1024]{0:T(1024)S(1)} %bitcast.63, f32[512]{0:T(512)S(1)} %bitcast.72, f32[1024]{0:T(1024)S(1)} %bitcast.60, ...), kind=kOutput, calls=%fused_computation.6.clone.1 | convolution fusion | flops 39845888 | bytes 2279424 | tf_op jit(solution)/shard_map/while/body/eval_jaxpr/dot_general | solution.py:102
  281.4 8.4 %convolution_bitcast_fusion.5 = f32[32,1024]{1,0:T(8,128)S(1)} fusion(bf16[32,512]{1,0:T(8,128)(2,1)S(1)} %get-tuple-element.270, f32[1024,512]{1,0:T(8,128)S(1)} %bitcast_divide_fusion.2, f32[512]{0:T(512)S(1)} %bitcast.68, f32[1024]{0:T(1024)S(1)} %bitcast.62, f32[512]{0:T(512)S(1)} %bitcast.71, f32[1024]{0:T(1024)S(1)} %bitcast.59, ...), kind=kOutput, calls=%fused_computation.7.clone.1 | convolution fusion | flops 39845888 | bytes 2279424 | tf_op jit(solution)/shard_map/while/body/eval_jaxpr/dot_general | solution.py:99
  289.8 8.5 %convolution_bitcast_fusion.4 = f32[32,1024]{1,0:T(8,128)S(1)} fusion(bf16[32,512]{1,0:T(8,128)(2,1)S(1)} %get-tuple-element.270, f32[1024,512]{1,0:T(8,128)S(1)} %bitcast_divide_fusion.2, f32[512]{0:T(512)S(1)} %bitcast.69, f32[1024]{0:T(1024)S(1)} %bitcast.63, f32[512]{0:T(512)S(1)} %bitcast.72, f32[1024]{0:T(1024)S(1)} %bitcast.60, ...), kind=kOutput, calls=%fused_computation.6.clone.1 | convolution fusion | flops 39845888 | bytes 2279424 | tf_op jit(solution)/shard_map/while/body/eval_jaxpr/dot_general | solution.py:102
  301.2 8.4 %convolution_bitcast_fusion.5 = f32[32,1024]{1,0:T(8,128)S(1)} fusion(bf16[32,512]{1,0:T(8,128)(2,1)S(1)} %get-tuple-element.270, f32[1024,512]{1,0:T(8,128)S(1)} %bitcast_divide_fusion.2, f32[512]{0:T(512)S(1)} %bitcast.68, f32[1024]{0:T(1024)S(1)} %bitcast.62, f32[512]{0:T(512)S(1)} %bitcast.71, f32[1024]{0:T(1024)S(1)} %bitcast.59, ...), kind=kOutput, calls=%fused_computation.7.clone.1 | convolution fusion | flops 39845888 | bytes 2279424 | tf_op jit(solution)/shard_map/while/body/eval_jaxpr/dot_general | solution.py:99
  309.6 8.5 %convolution_bitcast_fusion.4 = f32[32,1024]{1,0:T(8,128)S(1)} fusion(bf16[32,512]{1,0:T(8,128)(2,1)S(1)} %get-tuple-element.270, f32[1024,512]{1,0:T(8,128)S(1)} %bitcast_divide_fusion.2, f32[512]{0:T(512)S(1)} %bitcast.69, f32[1024]{0:T(1024)S(1)} %bitcast.63, f32[512]{0:T(512)S(1)} %bitcast.72, f32[1024]{0:T(1024)S(1)} %bitcast.60, ...), kind=kOutput, calls=%fused_computation.6.clone.1 | convolution fusion | flops 39845888 | bytes 2279424 | tf_op jit(solution)/shard_map/while/body/eval_jaxpr/dot_general | solution.py:102
  321.0 8.4 %convolution_bitcast_fusion.5 = f32[32,1024]{1,0:T(8,128)S(1)} fusion(bf16[32,512]{1,0:T(8,128)(2,1)S(1)} %get-tuple-element.270, f32[1024,512]{1,0:T(8,128)S(1)} %bitcast_divide_fusion.2, f32[512]{0:T(512)S(1)} %bitcast.68, f32[1024]{0:T(1024)S(1)} %bitcast.62, f32[512]{0:T(512)S(1)} %bitcast.71, f32[1024]{0:T(1024)S(1)} %bitcast.59, ...), kind=kOutput, calls=%fused_computation.7.clone.1 | convolution fusion | flops 39845888 | bytes 2279424 | tf_op jit(solution)/shard_map/while/body/eval_jaxpr/dot_general | solution.py:99
  329.4 8.5 %convolution_bitcast_fusion.4 = f32[32,1024]{1,0:T(8,128)S(1)} fusion(bf16[32,512]{1,0:T(8,128)(2,1)S(1)} %get-tuple-element.270, f32[1024,512]{1,0:T(8,128)S(1)} %bitcast_divide_fusion.2, f32[512]{0:T(512)S(1)} %bitcast.69, f32[1024]{0:T(1024)S(1)} %bitcast.63, f32[512]{0:T(512)S(1)} %bitcast.72, f32[1024]{0:T(1024)S(1)} %bitcast.60, ...), kind=kOutput, calls=%fused_computation.6.clone.1 | convolution fusion | flops 39845888 | bytes 2279424 | tf_op jit(solution)/shard_map/while/body/eval_jaxpr/dot_general | solution.py:102
  340.8 8.4 %convolution_bitcast_fusion.5 = f32[32,1024]{1,0:T(8,128)S(1)} fusion(bf16[32,512]{1,0:T(8,128)(2,1)S(1)} %get-tuple-element.270, f32[1024,512]{1,0:T(8,128)S(1)} %bitcast_divide_fusion.2, f32[512]{0:T(512)S(1)} %bitcast.68, f32[1024]{0:T(1024)S(1)} %bitcast.62, f32[512]{0:T(512)S(1)} %bitcast.71, f32[1024]{0:T(1024)S(1)} %bitcast.59, ...), kind=kOutput, calls=%fused_computation.7.clone.1 | convolution fusion | flops 39845888 | bytes 2279424 | tf_op jit(solution)/shard_map/while/body/eval_jaxpr/dot_general | solution.py:99
  349.2 8.5 %convolution_bitcast_fusion.4 = f32[32,1024]{1,0:T(8,128)S(1)} fusion(bf16[32,512]{1,0:T(8,128)(2,1)S(1)} %get-tuple-element.270, f32[1024,512]{1,0:T(8,128)S(1)} %bitcast_divide_fusion.2, f32[512]{0:T(512)S(1)} %bitcast.69, f32[1024]{0:T(1024)S(1)} %bitcast.63, f32[512]{0:T(512)S(1)} %bitcast.72, f32[1024]{0:T(1024)S(1)} %bitcast.60, ...), kind=kOutput, calls=%fused_computation.6.clone.1 | convolution fusion | flops 39845888 | bytes 2279424 | tf_op jit(solution)/shard_map/while/body/eval_jaxpr/dot_general | solution.py:102
  360.7 8.4 %convolution_bitcast_fusion.5 = f32[32,1024]{1,0:T(8,128)S(1)} fusion(bf16[32,512]{1,0:T(8,128)(2,1)S(1)} %get-tuple-element.270, f32[1024,512]{1,0:T(8,128)S(1)} %bitcast_divide_fusion.2, f32[512]{0:T(512)S(1)} %bitcast.68, f32[1024]{0:T(1024)S(1)} %bitcast.62, f32[512]{0:T(512)S(1)} %bitcast.71, f32[1024]{0:T(1024)S(1)} %bitcast.59, ...), kind=kOutput, calls=%fused_computation.7.clone.1 | convolution fusion | flops 39845888 | bytes 2279424 | tf_op jit(solution)/shard_map/while/body/eval_jaxpr/dot_general | solution.py:99
  369.1 8.5 %convolution_bitcast_fusion.4 = f32[32,1024]{1,0:T(8,128)S(1)} fusion(bf16[32,512]{1,0:T(8,128)(2,1)S(1)} %get-tuple-element.270, f32[1024,512]{1,0:T(8,128)S(1)} %bitcast_divide_fusion.2, f32[512]{0:T(512)S(1)} %bitcast.69, f32[1024]{0:T(1024)S(1)} %bitcast.63, f32[512]{0:T(512)S(1)} %bitcast.72, f32[1024]{0:T(1024)S(1)} %bitcast.60, ...), kind=kOutput, calls=%fused_computation.6.clone.1 | convolution fusion | flops 39845888 | bytes 2279424 | tf_op jit(solution)/shard_map/while/body/eval_jaxpr/dot_general | solution.py:102
  378.7 260.3 %reduce-scatter.2.cloned.1.call-done = f32[32,128]{1,0:T(8,128)} async-done(((f32[32,8192]{1,0:T(8,128)}), f32[32,128]{1,0:T(8,128)}) %reduce-scatter.2.cloned.1.call-update) | async-done | bytes 16400 | tf_op jit(solution)/shard_map/reduce_scatter | solution.py:112
  639.8 1.4 scatter_custom_fusion
  (127 shorter events, 40.5 us)
Async XLA Ops:
  7.2 631.8 %reduce-scatter.2.cloned.1.call-start = ((), (), s32[]{:S(2)}) async-start(), calls=%async_computation.1 | async-start | bytes 1064960 | tf_op jit(solution)/shard_map/reduce_scatter | solution.py:112
  8.2 18.8 %collective-permute-start.1 = (f32[32,1,8,128]{3,2,1,0:T(8,128)S(1)}, f32[32,1,8,128]{3,2,1,0:T(8,128)S(1)}, u32[]{:S(2)}, u32[]{:S(2)}) collective-permute-start(f32[32,1,8,128]{3,2,1,0:T(8,128)S(1)} %get-tuple-element.180), channel_id=1, source_target_pairs={{0,16},{16,32},{32,48},{48,64},{64,80},{80,96},{96,112},{112,128},... | collective-permute-start | bytes 393224 | tf_op jit(solution)/shard_map/ppermute | solution.py:26
  10.0 17.0 %collective-permute-start = (f32[32,1,8,128]{3,2,1,0:T(8,128)S(1)}, f32[32,1,8,128]{3,2,1,0:T(8,128)S(1)}, u32[]{:S(2)}, u32[]{:S(2)}) collective-permute-start(f32[32,1,8,128]{3,2,1,0:T(8,128)S(1)} %get-tuple-element.179), channel_id=1, source_target_pairs={{16,0},{32,16},{48,32},{64,48},{80,64},{96,80},{112,96},{128,112},... | collective-permute-start | bytes 393224 | tf_op jit(solution)/shard_map/ppermute | solution.py:27
  13.2 21.9 %copy-start.10 = (s32[128]{0:T(128)}, s32[128]{0:T(128)S(1)}, u32[]{:S(2)}) copy-start(s32[128]{0:T(128)S(1)} %compare_select_fusion) | copy-start | bytes 1540
  14.5 12.5 %copy-start = (f32[32,2,8,128]{3,2,1,0:T(8,128)S(1)}, f32[32,2,8,128]{3,2,1,0:T(8,128)}, u32[]{:S(2)}) copy-start(f32[32,2,8,128]{3,2,1,0:T(8,128)} %param.9) | copy-start | bytes 786436
  28.0 8.6 %collective-permute-start.2 = (f32[32,4,1,128]{3,0,2,1:T(8,128)S(1)}, f32[32,4,1,128]{3,0,2,1:T(8,128)S(1)}, u32[]{:S(2)}, u32[]{:S(2)}) collective-permute-start(f32[32,4,1,128]{3,0,2,1:T(8,128)S(1)} %copy.91), channel_id=1, source_target_pairs={{4,0},{8,4},{12,8},{5,1},{9,5},{13,9},{6,2},{10,6},{14,10},{7,3},{... | collective-permute-start | bytes 196616 | tf_op jit(solution)/shard_map/ppermute | solution.py:27
  29.3 7.7 %collective-permute-start.3 = (f32[32,4,1,128]{3,0,2,1:T(8,128)S(1)}, f32[32,4,1,128]{3,0,2,1:T(8,128)S(1)}, u32[]{:S(2)}, u32[]{:S(2)}) collective-permute-start(f32[32,4,1,128]{3,0,2,1:T(8,128)S(1)} %copy.92), channel_id=1, source_target_pairs={{0,4},{4,8},{8,12},{1,5},{5,9},{9,13},{2,6},{6,10},{10,14},{3,7},{... | collective-permute-start | bytes 196616 | tf_op jit(solution)/shard_map/ppermute | solution.py:26
  36.5 5.9 copy-start.7
  36.7 5.7 copy-start.2
  37.1 5.3 copy-start.3
  37.9 162.4 %collective-permute-start.4 = (f32[32,4,10,1]{0,2,3,1:T(8,128)}, f32[32,4,10,1]{0,2,3,1:T(8,128)}, u32[]{:S(2)}, u32[]{:S(2)}) collective-permute-start(f32[32,4,10,1]{0,2,3,1:T(8,128)} %get-tuple-element.170), channel_id=1, source_target_pairs={{1,0},{2,1},{3,2},{5,4},{6,5},{7,6},{9,8},{10,9},{11,10},{13,12},{... | collective-permute-start | bytes 15368 | tf_op jit(solution)/shard_map/ppermute | solution.py:27
  41.1 159.1 %collective-permute-start.5 = (f32[32,4,10,1]{0,2,3,1:T(8,128)}, f32[32,4,10,1]{0,2,3,1:T(8,128)}, u32[]{:S(2)}, u32[]{:S(2)}) collective-permute-start(f32[32,4,10,1]{0,2,3,1:T(8,128)} %get-tuple-element.171), channel_id=1, source_target_pairs={{0,1},{1,2},{2,3},{4,5},{5,6},{6,7},{8,9},{9,10},{10,11},{12,13},{... | collective-permute-start | bytes 15368 | tf_op jit(solution)/shard_map/ppermute | solution.py:26
  200.2 2.9 copy-start.4
  204.4 1.0 copy-start.5
  204.4 0.9 copy-start.6
  204.8 1.8 copy-start.8
  204.8 1.8 copy-start.9
  377.6 1.0 copy-start.1
Sparse Core Ops, SparseCore 0:
  378.8 260.1 reduce-scatter.1
where the time goes:
time: 651 us; the launch traced here: 649 us
  waiting for transfers between devices  261 us (40%)
  blocking collectives  163 us (25%)
  matrix products  135 us (21%)
  local copies, waits for them, and re-layouts  36.5 us (6%)
  other arithmetic  23.8 us (4%)
  starting transfers between devices  14.7 us (2%)
  between operations  14.4 us (2%)
    reduce_scatter x1, waiting for transfers between devices, on_device(): lax.psum_scatter(partial_value, ('grp', 'row'), scatter_dimension=1, tile...  260 us
    all_gather x1, blocking collectives, on_device(): targets = lax.all_gather(points, ('grp', 'row'), axis=1, tiled=True)  141 us
    dot_general x8, matrix products, one_block(): lax.dot_general(source_traces, tile_imag, CONTRACT, preferred_element_typ...  68.1 us
    dot_general x8, matrix products, one_block(): lax.dot_general(source_traces, tile_real, CONTRACT, preferred_element_typ...  67.3 us
  transfers between devices with their start and end apart: 7, of which 2 were waited for; matrix products, arithmetic and copies ran while one was open for 4% of the time, Pallas kernels for 0%

commit v1 on v0

--- a/solution.py
+++ b/solution.py
@@ -78,7 +78,10 @@
     cluster = points.shape[1]
     own_cols = lax.dynamic_index_in_dim(near_blocks, column_index, 1, keepdims=False)
     own_cols = lax.dynamic_index_in_dim(own_cols, group_index, 1, keepdims=False)
-    targets = lax.all_gather(points, ("grp", "row"), axis=1, tiled=True)
+    targets = jnp.concatenate(
+        lax.all_to_all(jnp.stack([points] * lax.axis_size(("grp", "row"))), ("grp", "row"), 0, 0),
+        axis=1,
+    )
     sources = lax.all_gather(points, "col", axis=1, tiled=True)
     source_traces = lax.all_gather(traces, "col", axis=1, tiled=True)
     target_count = targets.shape[1]

time: 651 us -> 534 us (0.82)
  blocking collectives: 163 us -> 22.4 us
  starting transfers between devices: 14.7 us -> 30 us
  waiting for transfers between devices: 261 us -> 268 us
    all_gather x1 -> x0, blocking collectives: 141 us -> none  [on_device(): targets = lax.all_gather(points, ('grp', 'row'), axis=1, tiled=True)]
    all_to_all x0 -> x1, starting transfers between devices: none -> 15.6 us  [on_device(): lax.all_to_all(jnp.stack([points] * lax.axis_size(('grp', 'row'))), ('grp...]
    reduce_scatter x1, waiting for transfers between devices: 260 us -> 268 us  [on_device(): lax.psum_scatter(partial_value, ('grp', 'row'), scatter_dimension=1, tile...]
  transfers between devices with their start and end apart: 7 -> 8, of which waited for: 2 -> 1; matrix products, arithmetic and copies ran while one was open for 4% -> 6% of each run, Pallas kernels for 0% -> 0%
where the time goes in v1:
time: 534 us; the launch traced here: 533 us
  waiting for transfers between devices  268 us (50%)
  matrix products  135 us (25%)
  local copies, waits for them, and re-layouts  37.9 us (7%)
  starting transfers between devices  30 us (6%)
  other arithmetic  23.8 us (4%)
  blocking collectives  22.4 us (4%)
  between operations  14.4 us (3%)
    reduce_scatter x1, waiting for transfers between devices, on_device(): lax.psum_scatter(partial_value, ('grp', 'row'), scatter_dimension=1, tile...  268 us
    dot_general x8, matrix products, one_block(): lax.dot_general(source_traces, tile_imag, CONTRACT, preferred_element_typ...  68.1 us
    dot_general x8, matrix products, one_block(): lax.dot_general(source_traces, tile_real, CONTRACT, preferred_element_typ...  67.3 us
    all_to_all x1, starting transfers between devices, on_device(): lax.all_to_all(jnp.stack([points] * lax.axis_size(('grp', 'row'))), ('grp...  15.6 us
    all_gather x1, blocking collectives, on_device(): source_traces = lax.all_gather(traces, 'col', axis=1, tiled=True)  12.1 us
    div x8, other arithmetic, kernel_tiles(): factor = listed / (FOUR_PI * distance)  11 us
    reshape x1, local copies, waits for them, and re-layouts, on_device(): near_list.reshape(group_count, column_count, group_count, column_count)  10.9 us
  transfers between devices with their start and end apart: 8, of which 1 were waited for; matrix products, arithmetic and copies ran while one was open for 6% of the time, Pallas kernels for 0%

profile of v1, /device:TPU:24, one launch (start us, length us, event | category | flops | bytes accessed | tf_op | source)
XLA Modules:
  0.0 532.6 jit_solution(10772994141709278477)
XLA Ops:
  8.2 1.7 collective-permute-start.1
  12.6 15.6 %all-to-all-start = ((f32[64,3,128]{2,1,0:T(4,128)}), f32[64,3,128]{2,1,0:T(4,128)}, u32[]{:S(2)}, u32[]{:S(2)}) async-start(f32[64,3,128]{2,1,0:T(4,128)} %stack.2), calls=%async_computation | async-start | bytes 262144 | tf_op jit(solution)/shard_map/all_to_all | solution.py:82
  31.5 10.9 %reshape.43 = s32[64,4,64,4]{3,2,1,0:T(8,128)} reshape(s32[256,256]{1,0:T(8,128)} %param.15) | data formatting | bytes 524288 | tf_op jit(solution)/shard_map/reshape | solution.py:77
  44.7 5.4 %collective-permute-start.3 = (f32[32,4,1,128]{3,0,2,1:T(8,128)S(1)}, f32[32,4,1,128]{3,0,2,1:T(8,128)S(1)}, u32[]{:S(2)}, u32[]{:S(2)}) collective-permute-start(f32[32,4,1,128]{3,0,2,1:T(8,128)S(1)} %copy.92), channel_id=1, source_target_pairs={{0,4},{4,8},{8,12},{1,5},{5,9},{9,13},{2,6},{6,10},{10,14},{3,7},{... | collective-permute-start | bytes 196616 | tf_op jit(solution)/shard_map/ppermute | solution.py:26
  50.2 1.6 constant_dynamic-slice_fusion.1
  53.6 3.2 collective-permute-start.4
  60.9 10.3 %all_gather.6 = f32[3,512]{1,0:T(4,128)S(1)} all-gather(f32[3,128]{1,0:T(4,128)} %param.12), channel_id=1, replica_groups=mesh['grp'=16,'row'=4,'col'=4] {'col'}, dimensions={1}, use_global_device_ids=true | all-gather | bytes 7680 | tf_op jit(solution)/shard_map/all_gather | solution.py:85
  71.2 2.3 copy.89
  73.5 2.3 copy.90
  75.8 2.9 fusion.7
  82.2 12.1 %all_gather.7 = bf16[32,512]{0,1:T(8,128)(2,1)S(1)} all-gather(bf16[32,128]{0,1:T(8,128)(2,1)S(1)} %fusion.16), channel_id=1, replica_groups=mesh['grp'=16,'row'=4,'col'=4] {'col'}, dimensions={1}, use_global_device_ids=true | all-gather | bytes 40960 | tf_op jit(solution)/shard_map/all_gather | solution.py:86
  94.5 158.8 %while.13 = (s32[]{:T(128)}, f32[32,8192]{1,0:T(8,128)S(1)}, f32[3,8192]{1,0:T(4,128)}, f32[3,512]{1,0:T(4,128)S(1)}, s32[64,4]{0,1:T(4,128)S(1)}, /*index=5*/bf...) while((s32[]{:T(128)}, f32[32,8192]{1,0:T(8,128)S(1)}, ...), condition=%wide.region_1.2_spmd, body=%wide.region_0.1_spmd.sunk | while | flops 85524528 | bytes 11561869 | solution.py:112
  97.5 8.4 %convolution_bitcast_fusion.5 = f32[32,1024]{1,0:T(8,128)S(1)} fusion(bf16[32,512]{1,0:T(8,128)(2,1)S(1)} %get-tuple-element.270, f32[1024,512]{1,0:T(8,128)S(1)} %bitcast_divide_fusion.2, f32[512]{0:T(512)S(1)} %bitcast.71, f32[1024]{0:T(1024)S(1)} %bitcast.65, f32[512]{0:T(512)S(1)} %bitcast.74, f32[1024]{0:T(1024)S(1)} %bitcast.62, ...), kind=kOutput, calls=%fused_computation.7.clone.1 | convolution fusion | flops 39845888 | bytes 2279424 | tf_op jit(solution)/shard_map/while/body/eval_jaxpr/dot_general | solution.py:102
  105.9 8.5 %convolution_bitcast_fusion.4 = f32[32,1024]{1,0:T(8,128)S(1)} fusion(bf16[32,512]{1,0:T(8,128)(2,1)S(1)} %get-tuple-element.270, f32[1024,512]{1,0:T(8,128)S(1)} %bitcast_divide_fusion.2, f32[512]{0:T(512)S(1)} %bitcast.72, f32[1024]{0:T(1024)S(1)} %bitcast.66, f32[512]{0:T(512)S(1)} %bitcast.75, f32[1024]{0:T(1024)S(1)} %bitcast.63, ...), kind=kOutput, calls=%fused_computation.6.clone.1 | convolution fusion | flops 39845888 | bytes 2279424 | tf_op jit(solution)/shard_map/while/body/eval_jaxpr/dot_general | solution.py:105
  116.0 1.4 bitcast_divide_fusion.2
  117.3 8.4 %convolution_bitcast_fusion.5 = f32[32,1024]{1,0:T(8,128)S(1)} fusion(bf16[32,512]{1,0:T(8,128)(2,1)S(1)} %get-tuple-element.270, f32[1024,512]{1,0:T(8,128)S(1)} %bitcast_divide_fusion.2, f32[512]{0:T(512)S(1)} %bitcast.71, f32[1024]{0:T(1024)S(1)} %bitcast.65, f32[512]{0:T(512)S(1)} %bitcast.74, f32[1024]{0:T(1024)S(1)} %bitcast.62, ...), kind=kOutput, calls=%fused_computation.7.clone.1 | convolution fusion | flops 39845888 | bytes 2279424 | tf_op jit(solution)/shard_map/while/body/eval_jaxpr/dot_general | solution.py:102
  125.7 8.5 %convolution_bitcast_fusion.4 = f32[32,1024]{1,0:T(8,128)S(1)} fusion(bf16[32,512]{1,0:T(8,128)(2,1)S(1)} %get-tuple-element.270, f32[1024,512]{1,0:T(8,128)S(1)} %bitcast_divide_fusion.2, f32[512]{0:T(512)S(1)} %bitcast.72, f32[1024]{0:T(1024)S(1)} %bitcast.66, f32[512]{0:T(512)S(1)} %bitcast.75, f32[1024]{0:T(1024)S(1)} %bitcast.63, ...), kind=kOutput, calls=%fused_computation.6.clone.1 | convolution fusion | flops 39845888 | bytes 2279424 | tf_op jit(solution)/shard_map/while/body/eval_jaxpr/dot_general | solution.py:105
  135.8 1.4 bitcast_divide_fusion.2
  137.2 8.4 %convolution_bitcast_fusion.5 = f32[32,1024]{1,0:T(8,128)S(1)} fusion(bf16[32,512]{1,0:T(8,128)(2,1)S(1)} %get-tuple-element.270, f32[1024,512]{1,0:T(8,128)S(1)} %bitcast_divide_fusion.2, f32[512]{0:T(512)S(1)} %bitcast.71, f32[1024]{0:T(1024)S(1)} %bitcast.65, f32[512]{0:T(512)S(1)} %bitcast.74, f32[1024]{0:T(1024)S(1)} %bitcast.62, ...), kind=kOutput, calls=%fused_computation.7.clone.1 | convolution fusion | flops 39845888 | bytes 2279424 | tf_op jit(solution)/shard_map/while/body/eval_jaxpr/dot_general | solution.py:102
  145.6 8.5 %convolution_bitcast_fusion.4 = f32[32,1024]{1,0:T(8,128)S(1)} fusion(bf16[32,512]{1,0:T(8,128)(2,1)S(1)} %get-tuple-element.270, f32[1024,512]{1,0:T(8,128)S(1)} %bitcast_divide_fusion.2, f32[512]{0:T(512)S(1)} %bitcast.72, f32[1024]{0:T(1024)S(1)} %bitcast.66, f32[512]{0:T(512)S(1)} %bitcast.75, f32[1024]{0:T(1024)S(1)} %bitcast.63, ...), kind=kOutput, calls=%fused_computation.6.clone.1 | convolution fusion | flops 39845888 | bytes 2279424 | tf_op jit(solution)/shard_map/while/body/eval_jaxpr/dot_general | solution.py:105
  157.0 8.4 %convolution_bitcast_fusion.5 = f32[32,1024]{1,0:T(8,128)S(1)} fusion(bf16[32,512]{1,0:T(8,128)(2,1)S(1)} %get-tuple-element.270, f32[1024,512]{1,0:T(8,128)S(1)} %bitcast_divide_fusion.2, f32[512]{0:T(512)S(1)} %bitcast.71, f32[1024]{0:T(1024)S(1)} %bitcast.65, f32[512]{0:T(512)S(1)} %bitcast.74, f32[1024]{0:T(1024)S(1)} %bitcast.62, ...), kind=kOutput, calls=%fused_computation.7.clone.1 | convolution fusion | flops 39845888 | bytes 2279424 | tf_op jit(solution)/shard_map/while/body/eval_jaxpr/dot_general | solution.py:102
  165.4 8.5 %convolution_bitcast_fusion.4 = f32[32,1024]{1,0:T(8,128)S(1)} fusion(bf16[32,512]{1,0:T(8,128)(2,1)S(1)} %get-tuple-element.270, f32[1024,512]{1,0:T(8,128)S(1)} %bitcast_divide_fusion.2, f32[512]{0:T(512)S(1)} %bitcast.72, f32[1024]{0:T(1024)S(1)} %bitcast.66, f32[512]{0:T(512)S(1)} %bitcast.75, f32[1024]{0:T(1024)S(1)} %bitcast.63, ...), kind=kOutput, calls=%fused_computation.6.clone.1 | convolution fusion | flops 39845888 | bytes 2279424 | tf_op jit(solution)/shard_map/while/body/eval_jaxpr/dot_general | solution.py:105
  176.8 8.4 %convolution_bitcast_fusion.5 = f32[32,1024]{1,0:T(8,128)S(1)} fusion(bf16[32,512]{1,0:T(8,128)(2,1)S(1)} %get-tuple-element.270, f32[1024,512]{1,0:T(8,128)S(1)} %bitcast_divide_fusion.2, f32[512]{0:T(512)S(1)} %bitcast.71, f32[1024]{0:T(1024)S(1)} %bitcast.65, f32[512]{0:T(512)S(1)} %bitcast.74, f32[1024]{0:T(1024)S(1)} %bitcast.62, ...), kind=kOutput, calls=%fused_computation.7.clone.1 | convolution fusion | flops 39845888 | bytes 2279424 | tf_op jit(solution)/shard_map/while/body/eval_jaxpr/dot_general | solution.py:102
  185.2 8.5 %convolution_bitcast_fusion.4 = f32[32,1024]{1,0:T(8,128)S(1)} fusion(bf16[32,512]{1,0:T(8,128)(2,1)S(1)} %get-tuple-element.270, f32[1024,512]{1,0:T(8,128)S(1)} %bitcast_divide_fusion.2, f32[512]{0:T(512)S(1)} %bitcast.72, f32[1024]{0:T(1024)S(1)} %bitcast.66, f32[512]{0:T(512)S(1)} %bitcast.75, f32[1024]{0:T(1024)S(1)} %bitcast.63, ...), kind=kOutput, calls=%fused_computation.6.clone.1 | convolution fusion | flops 39845888 | bytes 2279424 | tf_op jit(solution)/shard_map/while/body/eval_jaxpr/dot_general | solution.py:105
  196.7 8.4 %convolution_bitcast_fusion.5 = f32[32,1024]{1,0:T(8,128)S(1)} fusion(bf16[32,512]{1,0:T(8,128)(2,1)S(1)} %get-tuple-element.270, f32[1024,512]{1,0:T(8,128)S(1)} %bitcast_divide_fusion.2, f32[512]{0:T(512)S(1)} %bitcast.71, f32[1024]{0:T(1024)S(1)} %bitcast.65, f32[512]{0:T(512)S(1)} %bitcast.74, f32[1024]{0:T(1024)S(1)} %bitcast.62, ...), kind=kOutput, calls=%fused_computation.7.clone.1 | convolution fusion | flops 39845888 | bytes 2279424 | tf_op jit(solution)/shard_map/while/body/eval_jaxpr/dot_general | solution.py:102
  205.1 8.5 %convolution_bitcast_fusion.4 = f32[32,1024]{1,0:T(8,128)S(1)} fusion(bf16[32,512]{1,0:T(8,128)(2,1)S(1)} %get-tuple-element.270, f32[1024,512]{1,0:T(8,128)S(1)} %bitcast_divide_fusion.2, f32[512]{0:T(512)S(1)} %bitcast.72, f32[1024]{0:T(1024)S(1)} %bitcast.66, f32[512]{0:T(512)S(1)} %bitcast.75, f32[1024]{0:T(1024)S(1)} %bitcast.63, ...), kind=kOutput, calls=%fused_computation.6.clone.1 | convolution fusion | flops 39845888 | bytes 2279424 | tf_op jit(solution)/shard_map/while/body/eval_jaxpr/dot_general | solution.py:105
  216.5 8.4 %convolution_bitcast_fusion.5 = f32[32,1024]{1,0:T(8,128)S(1)} fusion(bf16[32,512]{1,0:T(8,128)(2,1)S(1)} %get-tuple-element.270, f32[1024,512]{1,0:T(8,128)S(1)} %bitcast_divide_fusion.2, f32[512]{0:T(512)S(1)} %bitcast.71, f32[1024]{0:T(1024)S(1)} %bitcast.65, f32[512]{0:T(512)S(1)} %bitcast.74, f32[1024]{0:T(1024)S(1)} %bitcast.62, ...), kind=kOutput, calls=%fused_computation.7.clone.1 | convolution fusion | flops 39845888 | bytes 2279424 | tf_op jit(solution)/shard_map/while/body/eval_jaxpr/dot_general | solution.py:102
  224.9 8.5 %convolution_bitcast_fusion.4 = f32[32,1024]{1,0:T(8,128)S(1)} fusion(bf16[32,512]{1,0:T(8,128)(2,1)S(1)} %get-tuple-element.270, f32[1024,512]{1,0:T(8,128)S(1)} %bitcast_divide_fusion.2, f32[512]{0:T(512)S(1)} %bitcast.72, f32[1024]{0:T(1024)S(1)} %bitcast.66, f32[512]{0:T(512)S(1)} %bitcast.75, f32[1024]{0:T(1024)S(1)} %bitcast.63, ...), kind=kOutput, calls=%fused_computation.6.clone.1 | convolution fusion | flops 39845888 | bytes 2279424 | tf_op jit(solution)/shard_map/while/body/eval_jaxpr/dot_general | solution.py:105
  236.3 8.4 %convolution_bitcast_fusion.5 = f32[32,1024]{1,0:T(8,128)S(1)} fusion(bf16[32,512]{1,0:T(8,128)(2,1)S(1)} %get-tuple-element.270, f32[1024,512]{1,0:T(8,128)S(1)} %bitcast_divide_fusion.2, f32[512]{0:T(512)S(1)} %bitcast.71, f32[1024]{0:T(1024)S(1)} %bitcast.65, f32[512]{0:T(512)S(1)} %bitcast.74, f32[1024]{0:T(1024)S(1)} %bitcast.62, ...), kind=kOutput, calls=%fused_computation.7.clone.1 | convolution fusion | flops 39845888 | bytes 2279424 | tf_op jit(solution)/shard_map/while/body/eval_jaxpr/dot_general | solution.py:102
  244.7 8.5 %convolution_bitcast_fusion.4 = f32[32,1024]{1,0:T(8,128)S(1)} fusion(bf16[32,512]{1,0:T(8,128)(2,1)S(1)} %get-tuple-element.270, f32[1024,512]{1,0:T(8,128)S(1)} %bitcast_divide_fusion.2, f32[512]{0:T(512)S(1)} %bitcast.72, f32[1024]{0:T(1024)S(1)} %bitcast.66, f32[512]{0:T(512)S(1)} %bitcast.75, f32[1024]{0:T(1024)S(1)} %bitcast.63, ...), kind=kOutput, calls=%fused_computation.6.clone.1 | convolution fusion | flops 39845888 | bytes 2279424 | tf_op jit(solution)/shard_map/while/body/eval_jaxpr/dot_general | solution.py:105
  254.3 268.1 %reduce-scatter.2.cloned.1.call-done = f32[32,128]{1,0:T(8,128)} async-done(((f32[32,8192]{1,0:T(8,128)}), f32[32,128]{1,0:T(8,128)}) %reduce-scatter.2.cloned.1.call-update) | async-done | bytes 16400 | tf_op jit(solution)/shard_map/reduce_scatter | solution.py:115
  523.2 1.4 scatter_custom_fusion
  (127 shorter events, 41.5 us)
Async XLA Ops:
  8.2 34.2 %collective-permute-start.1 = (f32[32,1,8,128]{3,2,1,0:T(8,128)S(1)}, f32[32,1,8,128]{3,2,1,0:T(8,128)S(1)}, u32[]{:S(2)}, u32[]{:S(2)}) collective-permute-start(f32[32,1,8,128]{3,2,1,0:T(8,128)S(1)} %get-tuple-element.180), channel_id=1, source_target_pairs={{0,16},{16,32},{32,48},{48,64},{64,80},{80,96},{96,112},{112,128},... | collective-permute-start | bytes 393224 | tf_op jit(solution)/shard_map/ppermute | solution.py:26
  9.9 32.5 %collective-permute-start = (f32[32,1,8,128]{3,2,1,0:T(8,128)S(1)}, f32[32,1,8,128]{3,2,1,0:T(8,128)S(1)}, u32[]{:S(2)}, u32[]{:S(2)}) collective-permute-start(f32[32,1,8,128]{3,2,1,0:T(8,128)S(1)} %get-tuple-element.179), channel_id=1, source_target_pairs={{16,0},{32,16},{48,32},{64,48},{80,64},{96,80},{112,96},{128,112},... | collective-permute-start | bytes 393224 | tf_op jit(solution)/shard_map/ppermute | solution.py:27
  12.6 81.8 %all-to-all-start = ((f32[64,3,128]{2,1,0:T(4,128)}), f32[64,3,128]{2,1,0:T(4,128)}, u32[]{:S(2)}, u32[]{:S(2)}) async-start(f32[64,3,128]{2,1,0:T(4,128)} %stack.2), calls=%async_computation | async-start | bytes 262144 | tf_op jit(solution)/shard_map/all_to_all | solution.py:82
  28.2 494.2 %reduce-scatter.2.cloned.1.call-start = ((), (), s32[]{:S(2)}) async-start(), calls=%async_computation.2 | async-start | bytes 1064960 | tf_op jit(solution)/shard_map/reduce_scatter | solution.py:115
  30.2 27.9 %copy-start.9 = (s32[128]{0:T(128)}, s32[128]{0:T(128)S(1)}, u32[]{:S(2)}) copy-start(s32[128]{0:T(128)S(1)} %compare_select_fusion) | copy-start | bytes 1540
  31.4 11.0 %copy-start = (f32[32,2,8,128]{3,2,1,0:T(8,128)S(1)}, f32[32,2,8,128]{3,2,1,0:T(8,128)}, u32[]{:S(2)}) copy-start(f32[32,2,8,128]{3,2,1,0:T(8,128)} %param.9) | copy-start | bytes 786436
  43.4 9.2 %collective-permute-start.2 = (f32[32,4,1,128]{3,0,2,1:T(8,128)S(1)}, f32[32,4,1,128]{3,0,2,1:T(8,128)S(1)}, u32[]{:S(2)}, u32[]{:S(2)}) collective-permute-start(f32[32,4,1,128]{3,0,2,1:T(8,128)S(1)} %copy.91), channel_id=1, source_target_pairs={{4,0},{8,4},{12,8},{5,1},{9,5},{13,9},{6,2},{10,6},{14,10},{7,3},{... | collective-permute-start | bytes 196616 | tf_op jit(solution)/shard_map/ppermute | solution.py:27
  44.7 8.0 %collective-permute-start.3 = (f32[32,4,1,128]{3,0,2,1:T(8,128)S(1)}, f32[32,4,1,128]{3,0,2,1:T(8,128)S(1)}, u32[]{:S(2)}, u32[]{:S(2)}) collective-permute-start(f32[32,4,1,128]{3,0,2,1:T(8,128)S(1)} %copy.92), channel_id=1, source_target_pairs={{0,4},{4,8},{8,12},{1,5},{5,9},{9,13},{2,6},{6,10},{10,14},{3,7},{... | collective-permute-start | bytes 196616 | tf_op jit(solution)/shard_map/ppermute | solution.py:26
  52.7 5.4 %copy-start.2 = (f32[32,4,1,128]{0,2,3,1:T(1,128)}, f32[32,4,1,128]{0,2,3,1:T(1,128)S(1)}, u32[]{:S(2)}) copy-start(f32[32,4,1,128]{0,2,3,1:T(1,128)S(1)} %copy.71) | copy-start | bytes 196612
  52.9 5.3 copy-start.3
  53.6 22.2 %collective-permute-start.4 = (f32[32,4,10,1]{0,2,3,1:T(8,128)}, f32[32,4,10,1]{0,2,3,1:T(8,128)}, u32[]{:S(2)}, u32[]{:S(2)}) collective-permute-start(f32[32,4,10,1]{0,2,3,1:T(8,128)} %get-tuple-element.170), channel_id=1, source_target_pairs={{1,0},{2,1},{3,2},{5,4},{6,5},{7,6},{9,8},{10,9},{11,10},{13,12},{... | collective-permute-start | bytes 15368 | tf_op jit(solution)/shard_map/ppermute | solution.py:27
  56.8 19.0 %collective-permute-start.5 = (f32[32,4,10,1]{0,2,3,1:T(8,128)}, f32[32,4,10,1]{0,2,3,1:T(8,128)}, u32[]{:S(2)}, u32[]{:S(2)}) collective-permute-start(f32[32,4,10,1]{0,2,3,1:T(8,128)} %get-tuple-element.171), channel_id=1, source_target_pairs={{0,1},{1,2},{2,3},{4,5},{5,6},{6,7},{8,9},{9,10},{10,11},{12,13},{... | collective-permute-start | bytes 15368 | tf_op jit(solution)/shard_map/ppermute | solution.py:26
  75.8 2.9 copy-start.4
  79.9 1.0 copy-start.5
  80.0 0.9 copy-start.6
  80.3 1.8 copy-start.7
  80.3 1.8 copy-start.8
  253.3 1.0 copy-start.1
Sparse Core Ops, SparseCore 0:
  254.5 267.9 reduce-scatter.1
